TPU v7x, 32 devices: a whole 2x2x4 slice. The times are simulated.
32 devices in a mesh: gx: 4 (over y, core), gy: 4 (over z), frame: 2 (over x).
Axes of the slice: x: 2, y: 2, z: 4, core: 2. Of those that a mesh axis runs over, the one named last changes fastest.
Arguments:
- features: bfloat16 [8, 8, 128, 128], P(('frame', 'gx'), 'gy'), parts along dimension 0, may hold values from -6 to 6
- positions: float32 [8, 8, 3, 128], P(('frame', 'gx'), 'gy'), parts along dimension 0, may hold values from 0 to 1
- bead_types: int32 [8, 8, 128], P(('frame', 'gx'), 'gy'), parts along dimension 0, may hold values from 0 to 15
- cell_counts: int32 [8, 8], P(('frame', 'gx'), 'gy'), parts along dimension 0, may hold values from 48 to 128
- w_value: bfloat16 [128, 128], replicated, may hold values from -0.5 to 0.5
- w_radial: float32 [8, 128], replicated, may hold values from -0.6 to 0.6
- type_gain: float32 [16, 128], replicated, may hold values from 0.1 to 1.9
- w_out: bfloat16 [128, 128], replicated, may hold values from -0.5 to 0.5
- cotangent: bfloat16 [8, 8, 128, 128], P(('frame', 'gx'), 'gy'), parts along dimension 0, may hold values from -6 to 6
Outputs:
- out_feat: bfloat16 [8, 8, 128, 128], P(('frame', 'gx'), 'gy'), parts along dimension 0
- grad_feat: bfloat16 [8, 8, 128, 128], P(('frame', 'gx'), 'gy'), parts along dimension 0
- grad_pos: float32 [8, 8, 3, 128], P(('frame', 'gx'), 'gy'), parts along dimension 0
- grad_wvalue: float32 [256, 128], P('frame'), parts along dimension 0
- grad_wradial: float32 [16, 128], P('frame'), parts along dimension 0
- grad_gain: float32 [32, 128], P('frame'), parts along dimension 0
- grad_wout: float32 [256, 128], P('frame'), parts along dimension 0
There are 2 independent parts, one for each index of `frame`. A program takes and returns all parts, laid end to end along the dimension named above; an argument that names none is the same for every part. Nothing has to cross between parts.
All inputs are finite; a program needn't handle non-finite values.
Results may differ from a plain program's by a relative error of at most 0.012.
Values may be sent and summed in bfloat16 or wider, within the bound.
No kernel may reach another device: no remote copies, remote signals or barrier semaphores. Data moves between devices by JAX's collectives and lax.ppermute only.
A program may use at most 64 MiB of HBM per device.

v0:
```python
import jax
import jax.numpy as jnp
from jax import lax
from jax.sharding import PartitionSpec as P

HZ = 6
soften = 0.01
stencil = [(-1, -1), (-1, 0), (-1, 1), (0, -1), (0, 0), (0, 1), (1, -1), (1, 0), (1, 1)]


def passed_along(block, axis, distance):
    devices = range(lax.axis_size(axis))
    route = [((i - distance) % len(devices), i) for i in devices]
    return lax.ppermute(block, axis, route)


def with_halo(block, sides, width):
    for axis, dim in sides:
        count = lax.axis_size(axis)
        forward = [(i, i + 1) for i in range(count - 1)]
        forward.append((count - 1, 0))
        backward = [(target, source) for source, target in forward]
        low = lax.ppermute(
            lax.slice_in_dim(block, block.shape[dim] - width, None, axis=dim), axis, forward
        )
        high = lax.ppermute(lax.slice_in_dim(block, 0, width, axis=dim), axis, backward)
        block = jnp.concatenate([low, block, high], axis=dim)
    return block


def pair_terms(pos_own, pos_near, shift_x, shift_y, is_self, basis_count):
    slot_count = pos_own.shape[-1]
    offsets = (float(shift_x), float(shift_y), 0.0)
    scales = (1.0, 1.0, float(HZ))
    deltas = [
        (pos_near[:, :, component, None, :] - pos_own[:, :, component, :, None]) * scales[component]
        + offsets[component]
        for component in range(3)
    ]
    dist_sq = deltas[0] * deltas[0] + deltas[1] * deltas[1] + deltas[2] * deltas[2]
    pair_mask = pos_own[:, :, 3, :, None] * pos_near[:, :, 3, None, :]
    if is_self:
        pair_mask = pair_mask * (1.0 - jnp.eye(slot_count, dtype=jnp.float32))
    radius = jnp.sqrt(dist_sq + soften)
    inside = jnp.maximum(1.0 - dist_sq, 0.0)
    envelope = inside * inside
    centres = jnp.arange(basis_count, dtype=jnp.float32) / (basis_count - 1)
    width_gamma = 0.5 * (basis_count - 1) ** 2
    offset_r = radius[:, :, None] - centres[None, None, :, None, None]
    gaussian = jnp.exp(-width_gamma * offset_r * offset_r)
    weights = ((pair_mask * envelope)[:, :, None] * gaussian).astype(jnp.bfloat16)
    slope_r2 = (
        pair_mask[:, :, None]
        * gaussian
        * (
            -2.0 * inside[:, :, None]
            - envelope[:, :, None] * width_gamma * offset_r / radius[:, :, None]
        )
    )
    scaled_deltas = [deltas[component] * scales[component] for component in range(3)]
    return (weights, slope_r2, scaled_deltas)


def fold_back(pos_accum, val_accum):
    row_count = pos_accum.shape[0] - 2
    for step_by, source, target in ((1, row_count + 1, 1), (-1, 0, row_count)):
        received = passed_along((pos_accum[source], val_accum[source]), "gx", step_by)
        pos_accum = pos_accum.at[target].add(received[0])
        val_accum = val_accum.at[target].add(received[1])
    pos_accum = pos_accum[1 : row_count + 1]
    val_accum = val_accum[1 : row_count + 1]
    col_count = pos_accum.shape[1] - 2
    for step_by, source, target in ((1, col_count + 1, 1), (-1, 0, col_count)):
        received = passed_along((pos_accum[:, source], val_accum[:, source]), "gy", step_by)
        pos_accum = pos_accum.at[:, target].add(received[0])
        val_accum = val_accum.at[:, target].add(received[1])
    return (pos_accum[:, 1 : col_count + 1], val_accum[:, 1 : col_count + 1])


def on_device(
    features, positions, bead_types, cell_counts, w_value, w_radial, type_gain, w_out, cotangent
):
    row_count, col_count, slot_count, channels = features.shape
    basis_count = w_radial.shape[0]
    valid_slot = (
        jnp.arange(slot_count, dtype=jnp.int32)[None, None, :] < cell_counts[:, :, None]
    ).astype(jnp.float32)
    pos_valid = jnp.concatenate([positions, valid_slot[:, :, None, :]], axis=2)
    flat_feat = features.reshape(-1, channels)
    projected = jnp.dot(flat_feat, w_value, preferred_element_type=jnp.float32)
    onehot = (
        bead_types.reshape(-1)[:, None] == jnp.arange(type_gain.shape[0], dtype=jnp.int32)[None, :]
    ).astype(jnp.float32)
    bead_gain = jnp.dot(onehot, type_gain, precision=lax.Precision.HIGHEST)
    carried = (
        (projected * bead_gain)
        .astype(jnp.bfloat16)
        .reshape(row_count, col_count, slot_count, channels)
    )
    pos_ext = with_halo(pos_valid, (("gx", 0), ("gy", 1)), 1)
    val_ext = with_halo(carried, (("gx", 0), ("gy", 1)), 1)

    def near_cells(extended, shift_x, shift_y):
        return extended[
            1 + shift_x : 1 + shift_x + row_count, 1 + shift_y : 1 + shift_y + col_count
        ]

    summed = jnp.zeros((row_count, col_count, basis_count, slot_count, channels), jnp.float32)
    for shift_x, shift_y in stencil:
        weights, slope_r2, deltas = pair_terms(
            pos_valid,
            near_cells(pos_ext, shift_x, shift_y),
            shift_x,
            shift_y,
            shift_x == 0 and shift_y == 0,
            basis_count,
        )
        summed = summed + jnp.einsum(
            "abkij,abjc->abkic",
            weights,
            near_cells(val_ext, shift_x, shift_y),
            preferred_element_type=jnp.float32,
        )
    aggregate = jnp.sum(summed * w_radial[None, None, :, None, :], axis=2)
    agg_half = aggregate.astype(jnp.bfloat16).reshape(-1, channels)
    pre_act = jnp.dot(agg_half, w_out, preferred_element_type=jnp.float32)
    sigmoid_act = jax.nn.sigmoid(pre_act)
    out_feat = (flat_feat.astype(jnp.float32) + pre_act * sigmoid_act).astype(jnp.bfloat16)
    grad_pre = (
        cotangent.reshape(-1, channels).astype(jnp.float32)
        * sigmoid_act
        * (1.0 + pre_act * (1.0 - sigmoid_act))
    ).astype(jnp.bfloat16)
    grad_wout = jnp.dot(agg_half.T, grad_pre, preferred_element_type=jnp.float32)
    grad_agg = (
        jnp.dot(grad_pre, w_out.T, preferred_element_type=jnp.float32)
        .astype(jnp.bfloat16)
        .reshape(row_count, col_count, slot_count, channels)
    )
    grad_wradial = jnp.sum(summed * grad_agg.astype(jnp.float32)[:, :, None], axis=(0, 1, 3))
    scaled = (grad_agg.astype(jnp.float32)[:, :, None] * w_radial[None, None, :, None, :]).astype(
        jnp.bfloat16
    )
    pos_accum = jnp.zeros((row_count + 2, col_count + 2, 3, slot_count), jnp.float32)
    val_accum = jnp.zeros((row_count + 2, col_count + 2, slot_count, channels), jnp.float32)
    for shift_x, shift_y in stencil:
        weights, slope_r2, deltas = pair_terms(
            pos_valid,
            near_cells(pos_ext, shift_x, shift_y),
            shift_x,
            shift_y,
            shift_x == 0 and shift_y == 0,
            basis_count,
        )
        weight_grad = jnp.einsum(
            "abkic,abjc->abkij",
            scaled,
            near_cells(val_ext, shift_x, shift_y),
            preferred_element_type=jnp.float32,
        )
        pair_pull = jnp.sum(weight_grad * slope_r2, axis=2)
        own_pull = jnp.stack(
            [-2.0 * jnp.sum(pair_pull * delta_one, axis=3) for delta_one in deltas], axis=2
        )
        far_pull = jnp.stack(
            [2.0 * jnp.sum(pair_pull * delta_one, axis=2) for delta_one in deltas], axis=2
        )
        far_value = jnp.einsum(
            "abkij,abkic->abjc", weights, scaled, preferred_element_type=jnp.float32
        )
        pos_accum = pos_accum.at[1 : row_count + 1, 1 : col_count + 1].add(own_pull)
        pos_accum = pos_accum.at[
            1 + shift_x : 1 + shift_x + row_count, 1 + shift_y : 1 + shift_y + col_count
        ].add(far_pull)
        val_accum = val_accum.at[
            1 + shift_x : 1 + shift_x + row_count, 1 + shift_y : 1 + shift_y + col_count
        ].add(far_value)
    grad_pos, grad_carried = fold_back(pos_accum, val_accum)
    flat_carried = grad_carried.reshape(-1, channels)
    grad_half = (flat_carried * bead_gain).astype(jnp.bfloat16)
    grad_feat = (
        cotangent.reshape(-1, channels).astype(jnp.float32)
        + jnp.dot(grad_half, w_value.T, preferred_element_type=jnp.float32)
    ).astype(jnp.bfloat16)
    grad_wvalue = jnp.dot(flat_feat.T, grad_half, preferred_element_type=jnp.float32)
    grad_gain = jnp.dot(onehot.T, flat_carried * projected, precision=lax.Precision.HIGHEST)
    summed_grads = lax.psum((grad_wvalue, grad_wradial, grad_gain, grad_wout), ("gx", "gy"))
    return (
        out_feat.reshape(row_count, col_count, slot_count, channels),
        grad_feat.reshape(row_count, col_count, slot_count, channels),
        grad_pos,
        summed_grads[0],
        summed_grads[1],
        summed_grads[2],
        summed_grads[3],
    )


def solution(mesh):
    return jax.shard_map(
        on_device,
        mesh=mesh,
        in_specs=(
            P(("frame", "gx"), "gy", None, None),
            P(("frame", "gx"), "gy", None, None),
            P(("frame", "gx"), "gy", None),
            P(("frame", "gx"), "gy"),
            P(),
            P(),
            P(),
            P(),
            P(("frame", "gx"), "gy", None, None),
        ),
        out_specs=(
            P(("frame", "gx"), "gy", None, None),
            P(("frame", "gx"), "gy", None, None),
            P(("frame", "gx"), "gy", None, None),
            P("frame", None),
            P("frame", None),
            P("frame", None),
            P("frame", None),
        ),
        check_vma=False,
    )
```

profile of v0, /device:TPU:8, one launch (start us, length us, event | category | flops | bytes accessed | tf_op | source)
XLA Modules:
  0.0 182.1 jit_solution(11763310224023146852)
XLA Ops:
  8.0 1.7 collective-permute-start.1
  10.8 1.7 collective-permute-start.4
  14.6 1.6 collective-permute-start.2
  16.7 1.6 collective-permute-done.2
  18.4 1.5 collective-permute-done.6
  21.9 1.6 collective-permute-start.5
  24.8 2.5 %collective-permute-done.5 = bf16[3,1,128,128]{3,2,1,0:T(8,128)(2,1)S(1)} collective-permute-done((bf16[3,1,128,128]{3,2,1,0:T(8,128)(2,1)S(1)}, bf16[3,1,128,128]{3,2,1,0:T(8,128)(2,1)S(1)}, u32[]{:S(2)}, u32[]{:S(2)}) %collective-permute-start.5) | collective-permute-done | bytes 98336 | tf_op jit(solution)/shard_map/ppermute | solution.py:23
  33.9 1.8 %fusion.16 = f32[3,4,128,128]{3,2,1,0:T(8,128)S(1)} fusion(f32[3,4,128,128]{3,2,1,0:T(8,128)S(1)} %scatter-add.104, s32[]{:T(128)} %bitcast.74, s32[]{:T(128)} %bitcast.75, f32[2,128,128]{2,1,0:T(8,128)S(1)} %bitcast_convert_fusion, f32[8,128]{1,0:T(8,128)S(1)} %copy-done.9, f32[2,128,128]{2,1,0:T(8,128)S(1)} %get-tuple-element.666, ...), kind=kOutput, calls=%fused_computation.63 | convolution fusion | flops 68976640 | bytes 659976 | tf_op jit(solution)/shard_map/abkij,abkic->abjc/dot_general | solution.py:168
  35.8 2.5 %fusion.19 = f32[3,4,128,128]{3,2,1,0:T(8,128)S(1)} fusion(f32[3,4,128,128]{3,2,1,0:T(8,128)S(1)} %fusion.16, s32[]{:T(128)} %bitcast.79, s32[]{:T(128)} %bitcast.80, f32[2,128,128]{2,1,0:T(8,128)S(1)} %bitcast_convert_fusion, f32[8,128]{1,0:T(8,128)S(1)} %copy-done.9, f32[2,128,128]{2,1,0:T(8,128)S(1)} %get-tuple-element.653, ...), kind=kOutput, calls=%fused_computation.66 | convolution fusion | flops 69009408 | bytes 659977 | tf_op jit(solution)/shard_map/abkij,abkic->abjc/dot_general | solution.py:168
  49.5 1.3 fusion.280
  50.8 1.4 scatter-add.126
  52.4 2.0 %add_select_fusion = f32[1,2,3,128]{3,1,2,0:T(2,128)S(1)} fusion(f32[3,4,3,128]{3,1,2,0:T(4,128)S(1)} %scatter-add.129, s32[]{:T(128)} %bitcast.79, s32[]{:T(128)} %bitcast.80, f32[1,2,1,128]{3,1,2,0:T(2,128)S(1)} %get-tuple-element.726, f32[1,2,1,128]{3,1,2,0:T(2,128)S(1)} %get-tuple-element.727, f32[1,2,1,128]{3,1,2,0:T(2,128)S(1)} %get-tuple-element.728, ...), kind=kLoop, calls=%fused_computation.451 | loop fusion | flops 3072 | bytes 9225 | tf_op jit(solution)/shard_map/select.53
  54.4 1.4 scatter-add.130
  57.3 1.7 collective-permute-start.13
  59.9 1.7 collective-permute-start.9
  63.0 2.3 %collective-permute-done.14 = f32[1,3,128]{2,0,1:T(1,128)S(1)} collective-permute-done((f32[1,3,128]{2,0,1:T(1,128)S(1)}, f32[1,3,128]{2,0,1:T(1,128)S(1)}, u32[]{:S(2)}, u32[]{:S(2)}) %collective-permute-start.14) | collective-permute-done | bytes 1568 | tf_op jit(solution)/shard_map/ppermute | solution.py:14
  65.3 1.5 collective-permute-done.8
  67.4 1.5 collective-permute-start.10
  69.5 2.9 %collective-permute-done.10 = f32[1,128,128]{2,1,0:T(8,128)S(1)} collective-permute-done((f32[1,128,128]{2,1,0:T(8,128)S(1)}, f32[1,128,128]{2,1,0:T(8,128)S(1)}, u32[]{:S(2)}, u32[]{:S(2)}) %collective-permute-start.10) | collective-permute-done | bytes 65568 | tf_op jit(solution)/shard_map/ppermute | solution.py:14
  72.5 2.7 %collective-permute-start.11 = (f32[1,128,128]{2,1,0:T(8,128)S(1)}, f32[1,128,128]{2,1,0:T(8,128)S(1)}, u32[]{:S(2)}, u32[]{:S(2)}) collective-permute-start(f32[1,128,128]{2,1,0:T(8,128)S(1)} %slice_bitcast_fusion.2), channel_id=1, source_target_pairs={{2,0},{4,2},{6,4},{0,6},{3,1},{5,3},{7,5},{1,7},{10,8},{12,10},{14... | collective-permute-start | bytes 196616 | tf_op jit(solution)/shard_map/ppermute | solution.py:14
  75.8 1.3 collective-permute-done.11
  79.1 58.6 %all-reduce.2 = (f32[8,128]{1,0:T(8,128)}, f32[16,128]{1,0:T(8,128)}) all-reduce(f32[8,128]{1,0:T(8,128)S(1)} %multiply_reduce_fusion, f32[16,128]{1,0:T(8,128)S(1)} %fusion.203), channel_id=1, replica_groups=mesh['gx'=4,'gy'=4,'frame'=2] {'gx','gy'}, use_global_device_ids=true, to_apply=%region_67.0 | all-reduce | flops 3072 | bytes 24576 | tf_op jit(solution)/shard_map/psum | solution.py:187
  137.7 35.2 %all-reduce.6.cloned.1.call-done = (f32[128,128]{0,1:T(8,128)}, f32[128,128]{1,0:T(8,128)}) async-done(((f32[128,128]{0,1:T(8,128)}, f32[128,128]{1,0:T(8,128)}), (f32[128,128]{0,1:T(8,128)}, f32[128,128]{1,0:T(8,128)})) %all-reduce.6.cloned.1.call-update) | async-done | bytes 131088 | tf_op jit(solution)/shard_map/psum | solution.py:187
  173.0 1.6 copy.44
  (179 shorter events, 33.2 us)
Async XLA Ops:
  7.2 24.9 %copy-start = (bf16[128,128]{1,0:T(8,128)(2,1)S(1)}, bf16[128,128]{1,0:T(8,128)(2,1)}, u32[]{:S(2)}) copy-start(bf16[128,128]{1,0:T(8,128)(2,1)} %param.86) | copy-start | bytes 98308
  7.2 2.5 %copy-start.8 = (f32[16,128]{1,0:T(8,128)S(1)}, f32[16,128]{1,0:T(8,128)}, u32[]{:S(2)}) copy-start(f32[16,128]{1,0:T(8,128)} %param.85) | copy-start | bytes 24580
  7.2 165.8 %all-reduce.6.cloned.1.call-start = ((), (), s32[]{:S(2)}) async-start(), calls=%async_computation | async-start | bytes 262144 | tf_op jit(solution)/shard_map/psum | solution.py:187
  7.9 1.8 copy-start.10
  7.9 6.7 %collective-permute-start = (f32[1,2,4,128]{3,1,2,0:T(2,128)S(1)}, f32[1,2,4,128]{3,1,2,0:T(2,128)S(1)}, u32[]{:S(2)}, u32[]{:S(2)}) collective-permute-start(f32[1,2,4,128]{3,1,2,0:T(2,128)S(1)} %pad_maximum_fusion.8), channel_id=1, source_target_pairs={{0,8},{8,16},{16,24},{24,0},{1,9},{9,17},{17,25},{25,1},{2,10},{10... | collective-permute-start | bytes 12296 | tf_op jit(solution)/shard_map/ppermute | solution.py:23
  8.0 6.6 %collective-permute-start.1 = (f32[1,2,4,128]{3,1,2,0:T(2,128)S(1)}, f32[1,2,4,128]{3,1,2,0:T(2,128)S(1)}, u32[]{:S(2)}, u32[]{:S(2)}) collective-permute-start(f32[1,2,4,128]{3,1,2,0:T(2,128)S(1)} %pad_maximum_fusion.8), channel_id=1, source_target_pairs={{8,0},{16,8},{24,16},{0,24},{9,1},{17,9},{25,17},{1,25},{10,2},{18... | collective-permute-start | bytes 12296 | tf_op jit(solution)/shard_map/ppermute | solution.py:26
  9.7 0.8 copy-start.3
  10.7 11.1 %collective-permute-start.3 = (bf16[1,2,128,128]{3,2,1,0:T(8,128)(2,1)S(1)}, bf16[1,2,128,128]{3,2,1,0:T(8,128)(2,1)S(1)}, u32[]{:S(2)}, u32[]{:S(2)}) collective-permute-start(bf16[1,2,128,128]{3,2,1,0:T(8,128)(2,1)S(1)} %bitcast.388), channel_id=1, source_target_pairs={{0,8},{8,16},{16,24},{24,0},{1,9},{9,17},{17,25},{25,1},{2,10},{10... | collective-permute-start | bytes 196616 | tf_op jit(solution)/shard_map/ppermute | solution.py:23
  10.8 11.0 %collective-permute-start.4 = (bf16[1,2,128,128]{3,2,1,0:T(8,128)(2,1)S(1)}, bf16[1,2,128,128]{3,2,1,0:T(8,128)(2,1)S(1)}, u32[]{:S(2)}, u32[]{:S(2)}) collective-permute-start(bf16[1,2,128,128]{3,2,1,0:T(8,128)(2,1)S(1)} %bitcast.389), channel_id=1, source_target_pairs={{8,0},{16,8},{24,16},{0,24},{9,1},{17,9},{25,17},{1,25},{10,2},{18... | collective-permute-start | bytes 196616 | tf_op jit(solution)/shard_map/ppermute | solution.py:26
  14.6 3.7 %collective-permute-start.2 = (f32[3,1,4,128]{3,1,2,0:T(1,128)S(1)}, f32[3,1,4,128]{3,1,2,0:T(1,128)S(1)}, u32[]{:S(2)}, u32[]{:S(2)}) collective-permute-start(f32[3,1,4,128]{3,1,2,0:T(1,128)S(1)} %get-tuple-element.616), channel_id=1, source_target_pairs={{0,2},{2,4},{4,6},{6,0},{1,3},{3,5},{5,7},{7,1},{8,10},{10,12},{12... | collective-permute-start | bytes 18440 | tf_op jit(solution)/shard_map/ppermute | solution.py:23
  16.3 3.6 %collective-permute-start.6 = (f32[3,1,4,128]{3,1,2,0:T(1,128)S(1)}, f32[3,1,4,128]{3,1,2,0:T(1,128)S(1)}, u32[]{:S(2)}, u32[]{:S(2)}) collective-permute-start(f32[3,1,4,128]{3,1,2,0:T(1,128)S(1)} %get-tuple-element.617), channel_id=1, source_target_pairs={{2,0},{4,2},{6,4},{0,6},{3,1},{5,3},{7,5},{1,7},{10,8},{12,10},{14... | collective-permute-start | bytes 18440 | tf_op jit(solution)/shard_map/ppermute | solution.py:26
  21.9 5.4 %collective-permute-start.5 = (bf16[3,1,128,128]{3,2,1,0:T(8,128)(2,1)S(1)}, bf16[3,1,128,128]{3,2,1,0:T(8,128)(2,1)S(1)}, u32[]{:S(2)}, u32[]{:S(2)}) collective-permute-start(bf16[3,1,128,128]{3,2,1,0:T(8,128)(2,1)S(1)} %get-tuple-element.582), channel_id=1, source_target_pairs={{0,2},{2,4},{4,6},{6,0},{1,3},{3,5},{5,7},{7,1},{8,10},{10,12},{12... | collective-permute-start | bytes 294920 | tf_op jit(solution)/shard_map/ppermute | solution.py:23
  23.5 5.3 %collective-permute-start.7 = (bf16[3,1,128,128]{3,2,1,0:T(8,128)(2,1)S(1)}, bf16[3,1,128,128]{3,2,1,0:T(8,128)(2,1)S(1)}, u32[]{:S(2)}, u32[]{:S(2)}) collective-permute-start(bf16[3,1,128,128]{3,2,1,0:T(8,128)(2,1)S(1)} %get-tuple-element.583), channel_id=1, source_target_pairs={{2,0},{4,2},{6,4},{0,6},{3,1},{5,3},{7,5},{1,7},{10,8},{12,10},{14... | collective-permute-start | bytes 294920 | tf_op jit(solution)/shard_map/ppermute | solution.py:26
  57.3 4.4 %collective-permute-start.12 = (f32[4,3,128]{2,0,1:T(4,128)S(1)}, f32[4,3,128]{2,0,1:T(4,128)S(1)}, u32[]{:S(2)}, u32[]{:S(2)}) collective-permute-start(f32[4,3,128]{2,0,1:T(4,128)S(1)} %get-tuple-element.590), channel_id=1, source_target_pairs={{24,0},{0,8},{8,16},{16,24},{25,1},{1,9},{9,17},{17,25},{26,2},{2,... | collective-permute-start | bytes 18440 | tf_op jit(solution)/shard_map/ppermute | solution.py:14
  57.3 4.3 %collective-permute-start.13 = (f32[4,3,128]{2,0,1:T(4,128)S(1)}, f32[4,3,128]{2,0,1:T(4,128)S(1)}, u32[]{:S(2)}, u32[]{:S(2)}) collective-permute-start(f32[4,3,128]{2,0,1:T(4,128)S(1)} %get-tuple-element.591), channel_id=1, source_target_pairs={{8,0},{16,8},{24,16},{0,24},{9,1},{17,9},{25,17},{1,25},{10,2},{18... | collective-permute-start | bytes 18440 | tf_op jit(solution)/shard_map/ppermute | solution.py:14
  59.9 6.9 %collective-permute-start.8 = (f32[4,128,128]{2,1,0:T(8,128)S(1)}, f32[4,128,128]{2,1,0:T(8,128)S(1)}, u32[]{:S(2)}, u32[]{:S(2)}) collective-permute-start(f32[4,128,128]{2,1,0:T(8,128)S(1)} %get-tuple-element.574), channel_id=1, source_target_pairs={{24,0},{0,8},{8,16},{16,24},{25,1},{1,9},{9,17},{17,25},{26,2},{2,... | collective-permute-start | bytes 786440 | tf_op jit(solution)/shard_map/ppermute | solution.py:14
  59.9 7.5 %collective-permute-start.9 = (f32[4,128,128]{2,1,0:T(8,128)S(1)}, f32[4,128,128]{2,1,0:T(8,128)S(1)}, u32[]{:S(2)}, u32[]{:S(2)}) collective-permute-start(f32[4,128,128]{2,1,0:T(8,128)S(1)} %get-tuple-element.575), channel_id=1, source_target_pairs={{8,0},{16,8},{24,16},{0,24},{9,1},{17,9},{25,17},{1,25},{10,2},{18... | collective-permute-start | bytes 786440 | tf_op jit(solution)/shard_map/ppermute | solution.py:14
  61.7 3.6 %collective-permute-start.14 = (f32[1,3,128]{2,0,1:T(1,128)S(1)}, f32[1,3,128]{2,0,1:T(1,128)S(1)}, u32[]{:S(2)}, u32[]{:S(2)}) collective-permute-start(f32[1,3,128]{2,0,1:T(1,128)S(1)} %slice_bitcast_fusion.7), channel_id=1, source_target_pairs={{6,0},{0,2},{2,4},{4,6},{7,1},{1,3},{3,5},{5,7},{14,8},{8,10},{10,... | collective-permute-start | bytes 4616 | tf_op jit(solution)/shard_map/ppermute | solution.py:14
  67.4 5.0 %collective-permute-start.10 = (f32[1,128,128]{2,1,0:T(8,128)S(1)}, f32[1,128,128]{2,1,0:T(8,128)S(1)}, u32[]{:S(2)}, u32[]{:S(2)}) collective-permute-start(f32[1,128,128]{2,1,0:T(8,128)S(1)} %slice_bitcast_fusion.3), channel_id=1, source_target_pairs={{6,0},{0,2},{2,4},{4,6},{7,1},{1,3},{3,5},{5,7},{14,8},{8,10},{10,... | collective-permute-start | bytes 196616 | tf_op jit(solution)/shard_map/ppermute | solution.py:14
  69.0 6.2 %collective-permute-start.15 = (f32[1,3,128]{2,0,1:T(1,128)S(1)}, f32[1,3,128]{2,0,1:T(1,128)S(1)}, u32[]{:S(2)}, u32[]{:S(2)}) collective-permute-start(f32[1,3,128]{2,0,1:T(1,128)S(1)} %slice_bitcast_fusion.6), channel_id=1, source_target_pairs={{2,0},{4,2},{6,4},{0,6},{3,1},{5,3},{7,5},{1,7},{10,8},{12,10},{14... | collective-permute-start | bytes 4616 | tf_op jit(solution)/shard_map/ppermute | solution.py:14
  72.5 4.6 %collective-permute-start.11 = (f32[1,128,128]{2,1,0:T(8,128)S(1)}, f32[1,128,128]{2,1,0:T(8,128)S(1)}, u32[]{:S(2)}, u32[]{:S(2)}) collective-permute-start(f32[1,128,128]{2,1,0:T(8,128)S(1)} %slice_bitcast_fusion.2), channel_id=1, source_target_pairs={{2,0},{4,2},{6,4},{0,6},{3,1},{5,3},{7,5},{1,7},{10,8},{12,10},{14... | collective-permute-start | bytes 196616 | tf_op jit(solution)/shard_map/ppermute | solution.py:14
  77.1 0.9 copy-start.4
  77.1 0.9 copy-start.6
  173.0 1.6 copy-start.7
  (6 other events, 4.4 us)
Sparse Core Ops, SparseCore 0:
  78.9 94.0 all-reduce.5
where the time goes:
time: 183 us; the launch traced here: 182 us
  blocking collectives  58.6 us (32%)
  waiting for transfers between devices  50.5 us (28%)
  matrix products  22.2 us (12%)
  starting transfers between devices  17.3 us (9%)
  between operations  15 us (8%)
  local copies, waits for them, and re-layouts  10.5 us (6%)
  other arithmetic  7.96 us (4%)
    psum x1, blocking collectives, on_device(): lax.psum((grad_wvalue, grad_wradial, grad_gain, grad_wout), ('gx', 'gy'))  58.6 us
    psum x1, waiting for transfers between devices, on_device(): lax.psum((grad_wvalue, grad_wradial, grad_gain, grad_wout), ('gx', 'gy'))  35.2 us
    ppermute x8, starting transfers between devices, passed_along(): return lax.ppermute(block, axis, route)  9.53 us
    ppermute x8, waiting for transfers between devices, passed_along(): return lax.ppermute(block, axis, route)  8.55 us
    dot_general x9, matrix products, on_device(): jnp.einsum('abkij,abkic->abjc', weights, scaled, preferred_element_type=j...  8.02 us
    dot_general x9, matrix products, on_device(): jnp.einsum('abkic,abjc->abkij', scaled, near_cells(val_ext, shift_x, shif...  5.84 us
    unnamed x28, local copies, waits for them, and re-layouts  4.4 us
    ppermute x4, starting transfers between devices, with_halo(): lax.ppermute(lax.slice_in_dim(block, 0, width, axis=dim), axis, backward)  4.36 us
  transfers between devices with their start and end apart: 17, of which 10 were waited for; matrix products, arithmetic and copies ran while one was open for 4% of the time, Pallas kernels for 0%

commit v1 on v0

--- a/solution.py
+++ b/solution.py
@@ -184,7 +184,7 @@
     ).astype(jnp.bfloat16)
     grad_wvalue = jnp.dot(flat_feat.T, grad_half, preferred_element_type=jnp.float32)
     grad_gain = jnp.dot(onehot.T, flat_carried * projected, precision=lax.Precision.HIGHEST)
-    summed_grads = lax.psum((grad_wvalue, grad_wradial, grad_gain, grad_wout), ("gx", "gy"))
+    summed_grads = lax.psum(lax.psum((grad_wvalue, grad_wradial, grad_gain, grad_wout), "gy"), "gx")
     return (
         out_feat.reshape(row_count, col_count, slot_count, channels),
         grad_feat.reshape(row_count, col_count, slot_count, channels),

time: 183 us -> 161 us (0.88)
  blocking collectives: 58.6 us -> 24.8 us
  waiting for transfers between devices: 50.5 us -> 60.3 us
    psum x1 -> x2, blocking collectives: 58.6 us -> 24.8 us  [the longest x1 14.1 us: on_device(): lax.psum((grad_wvalue, grad_wradial, grad_gain, grad_wout), 'gy')]
    psum x1 -> x2, waiting for transfers between devices: 35.2 us -> 45 us  [the longest x1 36.1 us: on_device(): lax.psum((grad_wvalue, grad_wradial, grad_gain, grad_wout), 'gy')]
  transfers between devices with their start and end apart: 17 -> 18, of which waited for: 10 -> 11; matrix products, arithmetic and copies ran while one was open for 4% -> 5% of each run, Pallas kernels for 0% -> 0%
where the time goes in v1:
time: 161 us; the launch traced here: 159 us
  waiting for transfers between devices  60.3 us (37%)
  blocking collectives  24.8 us (15%)
  matrix products  22.2 us (14%)
  starting transfers between devices  17.3 us (11%)
  between operations  15 us (9%)
  local copies, waits for them, and re-layouts  11.3 us (7%)
  other arithmetic  7.96 us (5%)
    psum x1, waiting for transfers between devices, on_device(): lax.psum((grad_wvalue, grad_wradial, grad_gain, grad_wout), 'gy')  36.1 us
    psum x1, blocking collectives, on_device(): lax.psum((grad_wvalue, grad_wradial, grad_gain, grad_wout), 'gy')  14.1 us
    psum x1, blocking collectives, on_device(): lax.psum(lax.psum((grad_wvalue, grad_wradial, grad_gain, grad_wout), 'gy'...  10.7 us
    ppermute x8, starting transfers between devices, passed_along(): return lax.ppermute(block, axis, route)  9.53 us
    psum x1, waiting for transfers between devices, on_device(): lax.psum(lax.psum((grad_wvalue, grad_wradial, grad_gain, grad_wout), 'gy'...  8.93 us
    ppermute x8, waiting for transfers between devices, passed_along(): return lax.ppermute(block, axis, route)  8.55 us
    dot_general x9, matrix products, on_device(): jnp.einsum('abkij,abkic->abjc', weights, scaled, preferred_element_type=j...  8.02 us
    dot_general x9, matrix products, on_device(): jnp.einsum('abkic,abjc->abkij', scaled, near_cells(val_ext, shift_x, shif...  5.84 us
  transfers between devices with their start and end apart: 18, of which 11 were waited for; matrix products, arithmetic and copies ran while one was open for 5% of the time, Pallas kernels for 0%

profile of v1, /device:TPU:8, one launch (start us, length us, event | category | flops | bytes accessed | tf_op | source)
XLA Modules:
  0.0 158.8 jit_solution(13378939690482541474)
XLA Ops:
  8.0 1.7 %collective-permute-start.1 = (f32[1,2,4,128]{3,1,2,0:T(2,128)S(1)}, f32[1,2,4,128]{3,1,2,0:T(2,128)S(1)}, u32[]{:S(2)}, u32[]{:S(2)}) collective-permute-start(f32[1,2,4,128]{3,1,2,0:T(2,128)S(1)} %pad_maximum_fusion.8), channel_id=1, source_target_pairs={{8,0},{16,8},{24,16},{0,24},{9,1},{17,9},{25,17},{1,25},{10,2},{18... | collective-permute-start | bytes 12296 | tf_op jit(solution)/shard_map/ppermute | solution.py:26
  10.8 1.7 %collective-permute-start.4 = (bf16[1,2,128,128]{3,2,1,0:T(8,128)(2,1)S(1)}, bf16[1,2,128,128]{3,2,1,0:T(8,128)(2,1)S(1)}, u32[]{:S(2)}, u32[]{:S(2)}) collective-permute-start(bf16[1,2,128,128]{3,2,1,0:T(8,128)(2,1)S(1)} %bitcast.389), channel_id=1, source_target_pairs={{8,0},{16,8},{24,16},{0,24},{9,1},{17,9},{25,17},{1,25},{10,2},{18... | collective-permute-start | bytes 196616 | tf_op jit(solution)/shard_map/ppermute | solution.py:26
  14.6 1.6 %collective-permute-start.2 = (f32[3,1,4,128]{3,1,2,0:T(1,128)S(1)}, f32[3,1,4,128]{3,1,2,0:T(1,128)S(1)}, u32[]{:S(2)}, u32[]{:S(2)}) collective-permute-start(f32[3,1,4,128]{3,1,2,0:T(1,128)S(1)} %get-tuple-element.620), channel_id=1, source_target_pairs={{0,2},{2,4},{4,6},{6,0},{1,3},{3,5},{5,7},{7,1},{8,10},{10,12},{12... | collective-permute-start | bytes 18440 | tf_op jit(solution)/shard_map/ppermute | solution.py:23
  16.7 1.6 %collective-permute-done.2 = f32[3,1,4,128]{3,1,2,0:T(1,128)S(1)} collective-permute-done((f32[3,1,4,128]{3,1,2,0:T(1,128)S(1)}, f32[3,1,4,128]{3,1,2,0:T(1,128)S(1)}, u32[]{:S(2)}, u32[]{:S(2)}) %collective-permute-start.2) | collective-permute-done | bytes 6176 | tf_op jit(solution)/shard_map/ppermute | solution.py:23
  18.4 1.5 collective-permute-done.6
  21.9 1.6 %collective-permute-start.5 = (bf16[3,1,128,128]{3,2,1,0:T(8,128)(2,1)S(1)}, bf16[3,1,128,128]{3,2,1,0:T(8,128)(2,1)S(1)}, u32[]{:S(2)}, u32[]{:S(2)}) collective-permute-start(bf16[3,1,128,128]{3,2,1,0:T(8,128)(2,1)S(1)} %get-tuple-element.586), channel_id=1, source_target_pairs={{0,2},{2,4},{4,6},{6,0},{1,3},{3,5},{5,7},{7,1},{8,10},{10,12},{12... | collective-permute-start | bytes 294920 | tf_op jit(solution)/shard_map/ppermute | solution.py:23
  24.8 2.5 %collective-permute-done.5 = bf16[3,1,128,128]{3,2,1,0:T(8,128)(2,1)S(1)} collective-permute-done((bf16[3,1,128,128]{3,2,1,0:T(8,128)(2,1)S(1)}, bf16[3,1,128,128]{3,2,1,0:T(8,128)(2,1)S(1)}, u32[]{:S(2)}, u32[]{:S(2)}) %collective-permute-start.5) | collective-permute-done | bytes 98336 | tf_op jit(solution)/shard_map/ppermute | solution.py:23
  33.9 1.8 %fusion.16 = f32[3,4,128,128]{3,2,1,0:T(8,128)S(1)} fusion(f32[3,4,128,128]{3,2,1,0:T(8,128)S(1)} %scatter-add.104, s32[]{:T(128)} %bitcast.74, s32[]{:T(128)} %bitcast.75, f32[2,128,128]{2,1,0:T(8,128)S(1)} %bitcast_convert_fusion, f32[8,128]{1,0:T(8,128)S(1)} %copy-done.9, f32[2,128,128]{2,1,0:T(8,128)S(1)} %get-tuple-element.670, ...), kind=kOutput, calls=%fused_computation.63 | convolution fusion | flops 68976640 | bytes 659976 | tf_op jit(solution)/shard_map/abkij,abkic->abjc/dot_general | solution.py:168
  35.8 2.5 %fusion.19 = f32[3,4,128,128]{3,2,1,0:T(8,128)S(1)} fusion(f32[3,4,128,128]{3,2,1,0:T(8,128)S(1)} %fusion.16, s32[]{:T(128)} %bitcast.79, s32[]{:T(128)} %bitcast.80, f32[2,128,128]{2,1,0:T(8,128)S(1)} %bitcast_convert_fusion, f32[8,128]{1,0:T(8,128)S(1)} %copy-done.9, f32[2,128,128]{2,1,0:T(8,128)S(1)} %get-tuple-element.657, ...), kind=kOutput, calls=%fused_computation.66 | convolution fusion | flops 69009408 | bytes 659977 | tf_op jit(solution)/shard_map/abkij,abkic->abjc/dot_general | solution.py:168
  50.8 1.4 scatter-add.126
  52.4 2.0 %add_select_fusion = f32[1,2,3,128]{3,1,2,0:T(2,128)S(1)} fusion(f32[3,4,3,128]{3,1,2,0:T(4,128)S(1)} %scatter-add.129, s32[]{:T(128)} %bitcast.79, s32[]{:T(128)} %bitcast.80, f32[1,2,1,128]{3,1,2,0:T(2,128)S(1)} %get-tuple-element.730, f32[1,2,1,128]{3,1,2,0:T(2,128)S(1)} %get-tuple-element.731, f32[1,2,1,128]{3,1,2,0:T(2,128)S(1)} %get-tuple-element.732, ...), kind=kLoop, calls=%fused_computation.451 | loop fusion | flops 3072 | bytes 9225 | tf_op jit(solution)/shard_map/select.53
  54.4 1.4 scatter-add.130
  57.3 1.7 %collective-permute-start.13 = (f32[4,3,128]{2,0,1:T(4,128)S(1)}, f32[4,3,128]{2,0,1:T(4,128)S(1)}, u32[]{:S(2)}, u32[]{:S(2)}) collective-permute-start(f32[4,3,128]{2,0,1:T(4,128)S(1)} %get-tuple-element.595), channel_id=1, source_target_pairs={{8,0},{16,8},{24,16},{0,24},{9,1},{17,9},{25,17},{1,25},{10,2},{18... | collective-permute-start | bytes 18440 | tf_op jit(solution)/shard_map/ppermute | solution.py:14
  59.9 1.7 %collective-permute-start.9 = (f32[4,128,128]{2,1,0:T(8,128)S(1)}, f32[4,128,128]{2,1,0:T(8,128)S(1)}, u32[]{:S(2)}, u32[]{:S(2)}) collective-permute-start(f32[4,128,128]{2,1,0:T(8,128)S(1)} %get-tuple-element.579), channel_id=1, source_target_pairs={{8,0},{16,8},{24,16},{0,24},{9,1},{17,9},{25,17},{1,25},{10,2},{18... | collective-permute-start | bytes 786440 | tf_op jit(solution)/shard_map/ppermute | solution.py:14
  63.0 2.3 %collective-permute-done.14 = f32[1,3,128]{2,0,1:T(1,128)S(1)} collective-permute-done((f32[1,3,128]{2,0,1:T(1,128)S(1)}, f32[1,3,128]{2,0,1:T(1,128)S(1)}, u32[]{:S(2)}, u32[]{:S(2)}) %collective-permute-start.14) | collective-permute-done | bytes 1568 | tf_op jit(solution)/shard_map/ppermute | solution.py:14
  65.3 1.5 collective-permute-done.8
  67.4 1.5 collective-permute-start.10
  69.5 2.9 %collective-permute-done.10 = f32[1,128,128]{2,1,0:T(8,128)S(1)} collective-permute-done((f32[1,128,128]{2,1,0:T(8,128)S(1)}, f32[1,128,128]{2,1,0:T(8,128)S(1)}, u32[]{:S(2)}, u32[]{:S(2)}) %collective-permute-start.10) | collective-permute-done | bytes 65568 | tf_op jit(solution)/shard_map/ppermute | solution.py:14
  72.5 2.7 %collective-permute-start.11 = (f32[1,128,128]{2,1,0:T(8,128)S(1)}, f32[1,128,128]{2,1,0:T(8,128)S(1)}, u32[]{:S(2)}, u32[]{:S(2)}) collective-permute-start(f32[1,128,128]{2,1,0:T(8,128)S(1)} %slice_bitcast_fusion.2), channel_id=1, source_target_pairs={{2,0},{4,2},{6,4},{0,6},{3,1},{5,3},{7,5},{1,7},{10,8},{12,10},{14... | collective-permute-start | bytes 196616 | tf_op jit(solution)/shard_map/ppermute | solution.py:14
  79.6 36.1 %all-reduce.9.cloned.1.call-done = (f32[128,128]{0,1:T(8,128)}, f32[128,128]{1,0:T(8,128)}) async-done(((f32[128,128]{0,1:T(8,128)}, f32[128,128]{1,0:T(8,128)}), (f32[128,128]{0,1:T(8,128)}, f32[128,128]{1,0:T(8,128)})) %all-reduce.9.cloned.1.call-update) | async-done | bytes 131088 | tf_op jit(solution)/shard_map/psum | solution.py:187
  116.0 14.1 %all-reduce.2 = (f32[8,128]{1,0:T(8,128)S(1)}, f32[16,128]{1,0:T(8,128)S(1)}) all-reduce(f32[8,128]{1,0:T(8,128)S(1)} %multiply_reduce_fusion, f32[16,128]{1,0:T(8,128)S(1)} %fusion.203), channel_id=1, replica_groups=mesh['gx'=4,'gy'=4,'frame'=2] {'gy'}, use_global_device_ids=true, to_apply=%region_68.0 | all-reduce | flops 3072 | bytes 24576 | tf_op jit(solution)/shard_map/psum | solution.py:187
  130.1 10.7 %all-reduce.4 = (f32[8,128]{1,0:T(8,128)}, f32[16,128]{1,0:T(8,128)}) all-reduce(f32[8,128]{1,0:T(8,128)S(1)} %get-tuple-element.567, f32[16,128]{1,0:T(8,128)S(1)} %get-tuple-element.568), channel_id=1, replica_groups=mesh['gx'=4,'gy'=4,'frame'=2] {'gx'}, use_global_device_ids=true, to_apply=%region_69.0 | all-reduce | flops 3072 | bytes 24576 | tf_op jit(solution)/shard_map/psum | solution.py:187
  140.8 8.9 %all-reduce.11.cloned.1.call-done = (f32[128,128]{0,1:T(8,128)}, f32[128,128]{1,0:T(8,128)}) async-done(((f32[128,128]{0,1:T(8,128)}, f32[128,128]{1,0:T(8,128)}), (f32[128,128]{0,1:T(8,128)}, f32[128,128]{1,0:T(8,128)})) %all-reduce.11.cloned.1.call-update) | async-done | bytes 131088 | tf_op jit(solution)/shard_map/psum | solution.py:187
  149.8 1.6 %copy.44 = f32[128,128]{1,0:T(8,128)} copy(f32[128,128]{0,1:T(8,128)} %get-tuple-element.573) | data formatting | bytes 131072
  (183 shorter events, 36.6 us)
Async XLA Ops:
  7.2 24.9 %copy-start = (bf16[128,128]{1,0:T(8,128)(2,1)S(1)}, bf16[128,128]{1,0:T(8,128)(2,1)}, u32[]{:S(2)}) copy-start(bf16[128,128]{1,0:T(8,128)(2,1)} %param.86) | copy-start | bytes 98308
  7.2 2.5 %copy-start.8 = (f32[16,128]{1,0:T(8,128)S(1)}, f32[16,128]{1,0:T(8,128)}, u32[]{:S(2)}) copy-start(f32[16,128]{1,0:T(8,128)} %param.85) | copy-start | bytes 24580
  7.2 108.5 %all-reduce.9.cloned.1.call-start = ((), (), s32[]{:S(2)}) async-start(), calls=%async_computation | async-start | bytes 262144 | tf_op jit(solution)/shard_map/psum | solution.py:187
  7.9 1.8 %copy-start.10 = (s32[1,2,128]{2,1,0:T(2,128)S(1)}, s32[1,2,128]{2,1,0:T(2,128)}, u32[]{:S(2)}) copy-start(s32[1,2,128]{2,1,0:T(2,128)} %param.81) | copy-start | bytes 3076
  7.9 6.7 %collective-permute-start = (f32[1,2,4,128]{3,1,2,0:T(2,128)S(1)}, f32[1,2,4,128]{3,1,2,0:T(2,128)S(1)}, u32[]{:S(2)}, u32[]{:S(2)}) collective-permute-start(f32[1,2,4,128]{3,1,2,0:T(2,128)S(1)} %pad_maximum_fusion.8), channel_id=1, source_target_pairs={{0,8},{8,16},{16,24},{24,0},{1,9},{9,17},{17,25},{25,1},{2,10},{10... | collective-permute-start | bytes 12296 | tf_op jit(solution)/shard_map/ppermute | solution.py:23
  8.0 6.6 %collective-permute-start.1 = (f32[1,2,4,128]{3,1,2,0:T(2,128)S(1)}, f32[1,2,4,128]{3,1,2,0:T(2,128)S(1)}, u32[]{:S(2)}, u32[]{:S(2)}) collective-permute-start(f32[1,2,4,128]{3,1,2,0:T(2,128)S(1)} %pad_maximum_fusion.8), channel_id=1, source_target_pairs={{8,0},{16,8},{24,16},{0,24},{9,1},{17,9},{25,17},{1,25},{10,2},{18... | collective-permute-start | bytes 12296 | tf_op jit(solution)/shard_map/ppermute | solution.py:26
  9.7 0.8 copy-start.3
  10.7 11.1 %collective-permute-start.3 = (bf16[1,2,128,128]{3,2,1,0:T(8,128)(2,1)S(1)}, bf16[1,2,128,128]{3,2,1,0:T(8,128)(2,1)S(1)}, u32[]{:S(2)}, u32[]{:S(2)}) collective-permute-start(bf16[1,2,128,128]{3,2,1,0:T(8,128)(2,1)S(1)} %bitcast.388), channel_id=1, source_target_pairs={{0,8},{8,16},{16,24},{24,0},{1,9},{9,17},{17,25},{25,1},{2,10},{10... | collective-permute-start | bytes 196616 | tf_op jit(solution)/shard_map/ppermute | solution.py:23
  10.8 11.0 %collective-permute-start.4 = (bf16[1,2,128,128]{3,2,1,0:T(8,128)(2,1)S(1)}, bf16[1,2,128,128]{3,2,1,0:T(8,128)(2,1)S(1)}, u32[]{:S(2)}, u32[]{:S(2)}) collective-permute-start(bf16[1,2,128,128]{3,2,1,0:T(8,128)(2,1)S(1)} %bitcast.389), channel_id=1, source_target_pairs={{8,0},{16,8},{24,16},{0,24},{9,1},{17,9},{25,17},{1,25},{10,2},{18... | collective-permute-start | bytes 196616 | tf_op jit(solution)/shard_map/ppermute | solution.py:26
  14.6 3.7 %collective-permute-start.2 = (f32[3,1,4,128]{3,1,2,0:T(1,128)S(1)}, f32[3,1,4,128]{3,1,2,0:T(1,128)S(1)}, u32[]{:S(2)}, u32[]{:S(2)}) collective-permute-start(f32[3,1,4,128]{3,1,2,0:T(1,128)S(1)} %get-tuple-element.620), channel_id=1, source_target_pairs={{0,2},{2,4},{4,6},{6,0},{1,3},{3,5},{5,7},{7,1},{8,10},{10,12},{12... | collective-permute-start | bytes 18440 | tf_op jit(solution)/shard_map/ppermute | solution.py:23
  16.3 3.6 %collective-permute-start.6 = (f32[3,1,4,128]{3,1,2,0:T(1,128)S(1)}, f32[3,1,4,128]{3,1,2,0:T(1,128)S(1)}, u32[]{:S(2)}, u32[]{:S(2)}) collective-permute-start(f32[3,1,4,128]{3,1,2,0:T(1,128)S(1)} %get-tuple-element.621), channel_id=1, source_target_pairs={{2,0},{4,2},{6,4},{0,6},{3,1},{5,3},{7,5},{1,7},{10,8},{12,10},{14... | collective-permute-start | bytes 18440 | tf_op jit(solution)/shard_map/ppermute | solution.py:26
  21.9 5.4 %collective-permute-start.5 = (bf16[3,1,128,128]{3,2,1,0:T(8,128)(2,1)S(1)}, bf16[3,1,128,128]{3,2,1,0:T(8,128)(2,1)S(1)}, u32[]{:S(2)}, u32[]{:S(2)}) collective-permute-start(bf16[3,1,128,128]{3,2,1,0:T(8,128)(2,1)S(1)} %get-tuple-element.586), channel_id=1, source_target_pairs={{0,2},{2,4},{4,6},{6,0},{1,3},{3,5},{5,7},{7,1},{8,10},{10,12},{12... | collective-permute-start | bytes 294920 | tf_op jit(solution)/shard_map/ppermute | solution.py:23
  23.5 5.3 %collective-permute-start.7 = (bf16[3,1,128,128]{3,2,1,0:T(8,128)(2,1)S(1)}, bf16[3,1,128,128]{3,2,1,0:T(8,128)(2,1)S(1)}, u32[]{:S(2)}, u32[]{:S(2)}) collective-permute-start(bf16[3,1,128,128]{3,2,1,0:T(8,128)(2,1)S(1)} %get-tuple-element.587), channel_id=1, source_target_pairs={{2,0},{4,2},{6,4},{0,6},{3,1},{5,3},{7,5},{1,7},{10,8},{12,10},{14... | collective-permute-start | bytes 294920 | tf_op jit(solution)/shard_map/ppermute | solution.py:26
  57.3 4.4 %collective-permute-start.12 = (f32[4,3,128]{2,0,1:T(4,128)S(1)}, f32[4,3,128]{2,0,1:T(4,128)S(1)}, u32[]{:S(2)}, u32[]{:S(2)}) collective-permute-start(f32[4,3,128]{2,0,1:T(4,128)S(1)} %get-tuple-element.594), channel_id=1, source_target_pairs={{24,0},{0,8},{8,16},{16,24},{25,1},{1,9},{9,17},{17,25},{26,2},{2,... | collective-permute-start | bytes 18440 | tf_op jit(solution)/shard_map/ppermute | solution.py:14
  57.3 4.3 %collective-permute-start.13 = (f32[4,3,128]{2,0,1:T(4,128)S(1)}, f32[4,3,128]{2,0,1:T(4,128)S(1)}, u32[]{:S(2)}, u32[]{:S(2)}) collective-permute-start(f32[4,3,128]{2,0,1:T(4,128)S(1)} %get-tuple-element.595), channel_id=1, source_target_pairs={{8,0},{16,8},{24,16},{0,24},{9,1},{17,9},{25,17},{1,25},{10,2},{18... | collective-permute-start | bytes 18440 | tf_op jit(solution)/shard_map/ppermute | solution.py:14
  59.9 6.9 %collective-permute-start.8 = (f32[4,128,128]{2,1,0:T(8,128)S(1)}, f32[4,128,128]{2,1,0:T(8,128)S(1)}, u32[]{:S(2)}, u32[]{:S(2)}) collective-permute-start(f32[4,128,128]{2,1,0:T(8,128)S(1)} %get-tuple-element.578), channel_id=1, source_target_pairs={{24,0},{0,8},{8,16},{16,24},{25,1},{1,9},{9,17},{17,25},{26,2},{2,... | collective-permute-start | bytes 786440 | tf_op jit(solution)/shard_map/ppermute | solution.py:14
  59.9 7.5 %collective-permute-start.9 = (f32[4,128,128]{2,1,0:T(8,128)S(1)}, f32[4,128,128]{2,1,0:T(8,128)S(1)}, u32[]{:S(2)}, u32[]{:S(2)}) collective-permute-start(f32[4,128,128]{2,1,0:T(8,128)S(1)} %get-tuple-element.579), channel_id=1, source_target_pairs={{8,0},{16,8},{24,16},{0,24},{9,1},{17,9},{25,17},{1,25},{10,2},{18... | collective-permute-start | bytes 786440 | tf_op jit(solution)/shard_map/ppermute | solution.py:14
  61.7 3.6 %collective-permute-start.14 = (f32[1,3,128]{2,0,1:T(1,128)S(1)}, f32[1,3,128]{2,0,1:T(1,128)S(1)}, u32[]{:S(2)}, u32[]{:S(2)}) collective-permute-start(f32[1,3,128]{2,0,1:T(1,128)S(1)} %slice_bitcast_fusion.7), channel_id=1, source_target_pairs={{6,0},{0,2},{2,4},{4,6},{7,1},{1,3},{3,5},{5,7},{14,8},{8,10},{10,... | collective-permute-start | bytes 4616 | tf_op jit(solution)/shard_map/ppermute | solution.py:14
  67.4 5.0 %collective-permute-start.10 = (f32[1,128,128]{2,1,0:T(8,128)S(1)}, f32[1,128,128]{2,1,0:T(8,128)S(1)}, u32[]{:S(2)}, u32[]{:S(2)}) collective-permute-start(f32[1,128,128]{2,1,0:T(8,128)S(1)} %slice_bitcast_fusion.3), channel_id=1, source_target_pairs={{6,0},{0,2},{2,4},{4,6},{7,1},{1,3},{3,5},{5,7},{14,8},{8,10},{10,... | collective-permute-start | bytes 196616 | tf_op jit(solution)/shard_map/ppermute | solution.py:14
  69.0 6.2 %collective-permute-start.15 = (f32[1,3,128]{2,0,1:T(1,128)S(1)}, f32[1,3,128]{2,0,1:T(1,128)S(1)}, u32[]{:S(2)}, u32[]{:S(2)}) collective-permute-start(f32[1,3,128]{2,0,1:T(1,128)S(1)} %slice_bitcast_fusion.6), channel_id=1, source_target_pairs={{2,0},{4,2},{6,4},{0,6},{3,1},{5,3},{7,5},{1,7},{10,8},{12,10},{14... | collective-permute-start | bytes 4616 | tf_op jit(solution)/shard_map/ppermute | solution.py:14
  72.5 4.6 %collective-permute-start.11 = (f32[1,128,128]{2,1,0:T(8,128)S(1)}, f32[1,128,128]{2,1,0:T(8,128)S(1)}, u32[]{:S(2)}, u32[]{:S(2)}) collective-permute-start(f32[1,128,128]{2,1,0:T(8,128)S(1)} %slice_bitcast_fusion.2), channel_id=1, source_target_pairs={{2,0},{4,2},{6,4},{0,6},{3,1},{5,3},{7,5},{1,7},{10,8},{12,10},{14... | collective-permute-start | bytes 196616 | tf_op jit(solution)/shard_map/ppermute | solution.py:14
  78.0 0.9 copy-start.6
  78.0 71.8 %all-reduce.11.cloned.1.call-start = ((), (), s32[]{:S(2)}) async-start(), calls=%async_computation.1 | async-start | bytes 262144 | tf_op jit(solution)/shard_map/psum | solution.py:187
  149.8 1.6 %copy-start.7 = (f32[128,128]{1,0:T(8,128)S(1)}, f32[128,128]{1,0:T(8,128)}, u32[]{:S(2)}) copy-start(f32[128,128]{1,0:T(8,128)} %get-tuple-element.766) | copy-start | bytes 196612
  (7 other events, 5.2 us)
Sparse Core Ops, SparseCore 0:
  78.1 37.5 all-reduce.8
  118.1 31.6 all-reduce.10
